TPU v7x, 32 devices: a whole 2x2x4 slice. The times are simulated.
32 devices in a mesh: ctx: 4 (over y, core), ep: 8 (over z, x).
Axes of the slice: x: 2, y: 2, z: 4, core: 2. Of those that a mesh axis runs over, the one named last changes fastest.
Arguments:
- resid: bfloat16 [4096, 2048], P(('ctx', 'ep')), may hold values from -12 to 12
- mixed_qkv: bfloat16 [4096, 4096], P(('ctx', 'ep')), may hold values from -6 to 6
- out_gate: bfloat16 [4096, 2048], P(('ctx', 'ep')), may hold values from -6 to 6
- beta: float32 [16, 4096], P(None, ('ctx', 'ep')), may hold values from 0.001 to 0.95
- log_decay: float32 [16, 4096], P(None, ('ctx', 'ep')), may hold values from -1 to 0
- conv_weight: float32 [4, 4096], replicated, may hold values from -3 to 3
- head_gain: float32 [128], replicated, may hold values from 0.25 to 1.75
- moe_gain: float32 [2048], replicated, may hold values from 0.25 to 1.75
- routes: int32 [4096, 3], P(('ctx', 'ep')), may hold values from 0 to 7, all different within a row; in each aligned block of 128 rows (0 to 127, 128 to 255, ...) at most 60 rows name the same one
- route_gates: float32 [4096, 3], P(('ctx', 'ep')), may hold values from 0.1 to 1
- w_in: bfloat16 [8, 2048, 1024], P('ep', 'ctx'), may hold values from -0.125 to 0.125
- w_out: bfloat16 [8, 512, 2048], P('ep', None, 'ctx'), may hold values from -0.25 to 0.25
Outputs:
- mixer_out: bfloat16 [4096, 2048], P(('ctx', 'ep'))
- layer_out: bfloat16 [4096, 2048], P(('ctx', 'ep'))
Inputs may be any that keep to these rules, and one draw needn't show every extreme that they name: `routes`: in the rows of one device no expert is named more than 60 times, a bound that some block reaches.
All inputs are finite; a program needn't handle non-finite values.
Results may differ from a plain program's by a relative error of at most 0.0037.
Values may be sent and summed in bfloat16 or wider, within the bound.
No kernel may reach another device: no remote copies, remote signals or barrier semaphores. Data moves between devices by JAX's collectives and lax.ppermute only.
A program may use at most 320 MiB of HBM per device.

v0:
```python
import jax
import jax.numpy as jnp
from jax import lax
from jax.sharding import PartitionSpec as P

HK = 8
VALUE_HEAD_SET = 16
DK = 128
DV = 128
MOE_H = 512
CONV = 4
TOPK = 3
TOK_DEV = 128
precise = lax.Precision.HIGHEST


def from_behind(value, axis, steps):
    count = lax.axis_size(axis)
    leading, last = (max(0, -steps), min(count, count - steps))
    return lax.ppermute(value, axis, [(source, source + steps) for source in range(leading, last)])


def entering(value, axis, join, neutral, backward):
    count, mine = (lax.axis_size(axis), lax.axis_index(axis))
    pieces = jax.tree.map(lambda part: lax.all_gather(part, axis), value)
    if backward:
        pieces = jax.tree.map(lambda part: part[::-1], pieces)
        mine = count - 1 - mine
    so_far = jax.tree.map(
        lambda part, zero: jnp.full_like(part, 0) + jnp.asarray(zero, part.dtype), value, neutral
    )

    def lap(position, so_far):
        longer = join(so_far, jax.tree.map(lambda part: part[position], pieces))
        return jax.tree.map(lambda new, old: jnp.where(position < mine, new, old), longer, so_far)

    return lax.fori_loop(0, count - 1, lap, so_far)


def short_conv(padded, conv_weight, row_count):
    qkv_data = padded.astype(jnp.float32)
    conv_sum = jnp.zeros((row_count, qkv_data.shape[1]), jnp.float32)
    for offset in range(conv_weight.shape[0]):
        conv_sum = conv_sum + qkv_data[offset : offset + row_count] * conv_weight[offset]
    return jax.nn.silu(conv_sum)


def local_terms(conv_out, beta, log_decay):
    row_count = conv_out.shape[0]
    head_group = VALUE_HEAD_SET // HK
    queries = conv_out[:, : HK * DK].reshape(row_count, HK, DK)
    keys_hat = conv_out[:, HK * DK : 2 * HK * DK].reshape(row_count, HK, DK)
    values = conv_out[:, 2 * HK * DK :].reshape(row_count, VALUE_HEAD_SET, DV)
    queries = (
        queries
        * lax.rsqrt(jnp.sum(queries * queries, axis=-1, keepdims=True) + 1e-06)
        * DK ** (-0.5)
    )
    keys_hat = keys_hat * lax.rsqrt(jnp.sum(keys_hat * keys_hat, axis=-1, keepdims=True) + 1e-06)
    queries = jnp.repeat(queries, head_group, axis=1).transpose(1, 0, 2)
    keys_hat = jnp.repeat(keys_hat, head_group, axis=1).transpose(1, 0, 2)
    values = values.transpose(1, 0, 2)
    cumulative = jnp.cumsum(log_decay, axis=1)
    positions = jnp.arange(row_count)
    strict_mask = (positions[:, None] > positions[None, :])[None]
    causal_mask = (positions[:, None] >= positions[None, :])[None]
    log_gap = cumulative[:, :, None] - cumulative[:, None, :]
    fading = jnp.where(causal_mask, jnp.exp(jnp.where(causal_mask, log_gap, 0.0)), 0.0)
    key_key = jnp.einsum("htd,hsd->hts", keys_hat, keys_hat, precision=precise)
    mixing = jnp.where(strict_mask, beta[:, :, None] * fading * key_key, 0.0)
    identity_t = jnp.eye(row_count, dtype=jnp.float32)
    weights_solved = lax.linalg.triangular_solve(
        identity_t[None] + mixing, identity_t[None] * beta[:, :, None], left_side=True, lower=True
    )
    block_fade = jnp.exp(cumulative)
    tail_fade = jnp.exp(cumulative[:, -1:] - cumulative)
    fresh_vals = jnp.einsum("hts,hsv->htv", weights_solved, values, precision=precise)
    carried = jnp.einsum(
        "hts,hsk->htk", weights_solved, block_fade[:, :, None] * keys_hat, precision=precise
    )
    faded_keys = tail_fade[:, :, None] * keys_hat
    transition = block_fade[:, -1][:, None, None] * jnp.eye(DK, dtype=jnp.float32)[
        None
    ] - jnp.einsum("htj,htk->hjk", carried, faded_keys, precision=precise)
    state_add = jnp.einsum("htv,htk->hvk", fresh_vals, faded_keys, precision=precise)
    scores = fading * jnp.einsum("htd,hsd->hts", queries, keys_hat, precision=precise)
    return (queries, block_fade, scores, fresh_vals, carried, transition, state_add)


def head_outputs(queries, block_fade, scores, fresh_vals, carried, start_state):
    new_vals = fresh_vals - jnp.einsum("htk,hvk->htv", carried, start_state, precision=precise)
    from_state = jnp.einsum("htk,hvk->htv", queries, start_state, precision=precise)
    return block_fade[:, :, None] * from_state + jnp.einsum(
        "hts,hsv->htv", scores, new_vals, precision=precise
    )


def gated_norm(head_out, out_gate, head_gain):
    row_count = head_out.shape[1]
    per_token = head_out.transpose(1, 0, 2)
    scaled = (
        per_token
        * lax.rsqrt(jnp.mean(per_token * per_token, axis=-1, keepdims=True) + 1e-06)
        * head_gain
    )
    gate_vals = out_gate.astype(jnp.float32).reshape(row_count, VALUE_HEAD_SET, DV)
    return (
        (scaled * jax.nn.silu(gate_vals))
        .reshape(row_count, VALUE_HEAD_SET * DV)
        .astype(jnp.bfloat16)
    )


def compose(earlier, later):
    first_map, first_add = earlier
    second_map, second_add = later
    joined_map = jnp.einsum("hij,hjk->hik", first_map, second_map, precision=precise)
    joined_add = jnp.einsum("hvj,hjk->hvk", first_add, second_map, precision=precise) + second_add
    return (joined_map, joined_add)


def compose_back(higher, lower):
    return compose(lower, higher)


def expert_mlp(token_rows, weight_in, weight_out):
    projected = jnp.dot(token_rows, weight_in, preferred_element_type=jnp.float32)
    activated = (jax.nn.silu(projected[:, :MOE_H]) * projected[:, MOE_H:]).astype(jnp.bfloat16)
    return jnp.dot(activated, weight_out, preferred_element_type=jnp.float32).astype(jnp.bfloat16)


def shards(
    resid,
    mixed_qkv,
    out_gate,
    beta,
    log_decay,
    conv_weight,
    head_gain,
    moe_gain,
    routes,
    route_gates,
    w_in,
    w_out,
):
    row_count = mixed_qkv.shape[0]
    rim_rows = from_behind(mixed_qkv[row_count - CONV + 1 :], ("ctx", "ep"), 1)
    conv_out = short_conv(jnp.concatenate([rim_rows, mixed_qkv], axis=0), conv_weight, row_count)
    queries, block_fade, scores, fresh_vals, carried, transition, state_add = local_terms(
        conv_out, beta, log_decay
    )
    neutral = (
        jnp.broadcast_to(jnp.eye(DK, dtype=jnp.float32)[None], transition.shape),
        jnp.zeros_like(state_add),
    )
    within_group = entering((transition, state_add), "ep", compose, neutral, False)
    through_own = compose(within_group, (transition, state_add))
    after_own = entering((transition, state_add), "ep", compose_back, neutral, True)
    group_whole = compose(through_own, after_own)
    before_group = entering(group_whole, "ctx", compose, neutral, False)
    start_state = compose(before_group, within_group)[1]
    head_out = head_outputs(queries, block_fade, scores, fresh_vals, carried, start_state)
    mixer_out = gated_norm(head_out, out_gate, head_gain)
    residual_mid = resid.astype(jnp.float32) + mixer_out.astype(jnp.float32)
    moe_input = (
        residual_mid
        * lax.rsqrt(jnp.mean(residual_mid * residual_mid, axis=-1, keepdims=True) + 1e-06)
        * moe_gain
    ).astype(jnp.bfloat16)
    expert_count = lax.axis_size("ep")
    capacity = max(2, (5 * TOK_DEV * TOPK + 4 * expert_count - 1) // (4 * expert_count))
    slot_count = expert_count * capacity
    width = moe_input.shape[1]
    flat_routes = routes.reshape(-1)
    one_hot = (flat_routes[:, None] == jnp.arange(expert_count)[None, :]).astype(jnp.int32)
    earlier_same = jnp.cumsum(one_hot, axis=0) - one_hot
    slot_rank = jnp.sum(earlier_same * one_hot, axis=1)
    slot_ids = flat_routes * capacity + slot_rank
    selector = (slot_ids[None, :] == jnp.arange(slot_count)[:, None]).astype(jnp.int32)
    selector = jnp.sum(selector.reshape(slot_count, row_count, TOPK), axis=2).astype(jnp.bfloat16)
    send_rows = jnp.dot(selector, moe_input, preferred_element_type=jnp.float32).astype(
        jnp.bfloat16
    )
    send_rows = send_rows.reshape(expert_count, capacity, width)
    whole_in, whole_out = (
        lax.all_gather(w_in, "ctx", axis=1, tiled=True),
        lax.all_gather(w_out, "ctx", axis=2, tiled=True),
    )
    slot_rows = lax.all_to_all(send_rows, "ep", split_axis=0, concat_axis=0, tiled=True)
    flat_rows = slot_rows.reshape(-1, width)
    result_rows = expert_mlp(flat_rows, whole_in[0], whole_out[0]).reshape(slot_rows.shape)
    returned = lax.all_to_all(result_rows, "ep", split_axis=0, concat_axis=0, tiled=True)
    returned_flat = returned.reshape(slot_count, width)
    picked_rows = returned_flat[slot_ids].reshape(row_count, TOPK, width)
    combined = jnp.einsum("tk,tkd->td", route_gates, picked_rows.astype(jnp.float32))
    layer_out = (residual_mid + combined).astype(jnp.bfloat16)
    return (mixer_out, layer_out)


def solution(mesh):
    return jax.shard_map(
        shards,
        mesh=mesh,
        in_specs=(
            P(("ctx", "ep"), None),
            P(("ctx", "ep"), None),
            P(("ctx", "ep"), None),
            P(None, ("ctx", "ep")),
            P(None, ("ctx", "ep")),
            P(),
            P(),
            P(),
            P(("ctx", "ep"), None),
            P(("ctx", "ep"), None),
            P("ep", "ctx", None),
            P("ep", None, "ctx"),
        ),
        out_specs=(P(("ctx", "ep"), None), P(("ctx", "ep"), None)),
        check_vma=False,
    )
```

profile of v0, /device:TPU:0, one launch (start us, length us, event | category | flops | bytes accessed | tf_op | source)
XLA Modules:
  0.0 815.7 jit_solution(8747101318717336057)
XLA Ops:
  8.1 4.8 collective-permute-start
  18.2 4.6 divide_multiply_fusion
  28.0 158.6 %custom-call.3 = f32[16,1,128,128]{2,3,1,0:T(8,128)} custom-call(f32[16,1,128,128]{3,2,1,0:T(8,128)} %fusion.39), custom_call_target="InvertDiagBlocksLowerTriangular" | custom-call | tf_op jit(solution)/shard_map/triangular_solve | solution.py:72
  204.0 119.6 %all-gather.17.cloned.1.call-done = f32[128,128,128]{2,1,0:T(8,128)} async-done(((f32[16,128,128]{2,1,0:T(8,128)}), f32[128,128,128]{2,1,0:T(8,128)}) %all-gather.17.cloned.1.call-update) | async-done | bytes 8388624 | tf_op jit(solution)/shard_map/all_gather | solution.py:25
  323.6 7.7 rev.7
  331.4 117.5 %all-gather.15.cloned.1.call-done = f32[128,128,128]{2,1,0:T(8,128)} async-done(((f32[16,128,128]{2,1,0:T(8,128)}), f32[128,128,128]{2,1,0:T(8,128)}) %all-gather.15.cloned.1.call-update) | async-done | bytes 8388624 | tf_op jit(solution)/shard_map/all_gather | solution.py:25
  448.9 7.7 rev.6
  456.7 71.4 %while.46 = (s32[]{:T(128)}, f32[16,128,128]{1,2,0:T(8,128)S(1)}, f32[16,128,128]{1,2,0:T(8,128)}, s32[]{:T(128)}, f32[8,16,128,128]{3,2,1,0:T(8,128)}, /*index=5*/f32[8,16,128,128]{3,2,1,0:T(8,128)}, s32[]{:T(128)}, s32[]{:T(128)}) while((s32[]{:T(128)}, f32[16,128,128]{1,2,0:T(8,128)S(1)}, f32[16,128,128]{1,2,0:T(8,128)}, ...), condition=%wide.region_4.5_spmd.clone, body=%wide.region_3.4_spmd.clone.sunk | while | flops 806617088 | bytes 17828460 | solution.py:37
  459.6 4.1 fusion.118
  480.0 4.1 fusion.118
  490.2 4.1 fusion.118
  510.6 4.1 fusion.118
  520.8 4.1 fusion.118
  528.1 4.8 convolution_add_fusion.2
  533.0 37.2 %while.47 = (s32[]{:T(128)}, f32[16,128,128]{2,1,0:T(8,128)S(1)}, f32[16,128,128]{2,1,0:T(8,128)S(1)}, s32[]{:T(128)}, f32[8,16,128,128]{3,2,1,0:T(8,128)}, /*in...) while((s32[]{:T(128)}, f32[16,128,128]{2,1,0:T(8,128)S(1)}, f32[16,128,128]{2,1,0:T(8,128)S(1)}, ...), condition=%wide.region_6.7_spmd.clone, body=%wide.region_5.6_spmd.clone.sunk | while | flops 806354944 | bytes 10486890 | solution.py:37
  592.2 14.2 %all-gather.21.cloned.1.call-done = f32[64,128,128]{2,1,0:T(8,128)} async-done(((f32[16,128,128]{2,1,0:T(8,128)}), f32[64,128,128]{2,1,0:T(8,128)}) %all-gather.21.cloned.1.call-update) | async-done | bytes 4194320 | tf_op jit(solution)/shard_map/all_gather | solution.py:25
  606.4 35.9 %all-gather.19.cloned.1.call-done = f32[64,128,128]{2,1,0:T(8,128)} async-done(((f32[16,128,128]{2,1,0:T(8,128)}), f32[64,128,128]{2,1,0:T(8,128)}) %all-gather.19.cloned.1.call-update) | async-done | bytes 4194320 | tf_op jit(solution)/shard_map/all_gather | solution.py:25
  642.3 21.5 %while.48 = (s32[]{:T(128)}, f32[16,128,128]{1,2,0:T(8,128)}, s32[]{:T(128)}, f32[4,16,128,128]{3,2,1,0:T(8,128)}, f32[4,16,128,128]{3,2,1,0:T(8,128)}, /*index=5*/s32[]{:T(128)}, s32[]{:T(128)}) while((s32[]{:T(128)}, f32[16,128,128]{1,2,0:T(8,128)}, s32[]{:T(128)}, f32[4,16,128,128]{3,2,1,0:T(8,128)}, ...), condition=%wide.region_8.9_spmd.clone, body=%wide.region_7.8_spmd.clone.sunk | while | flops 403701760 | bytes 11536483 | solution.py:37
  652.3 4.2 fusion.125
  677.6 5.8 all-to-all-start
  684.0 48.1 %all-to-all-done = bf16[8,60,2048]{2,1,0:T(8,128)(2,1)S(1)} async-done(((bf16[8,60,2048]{2,1,0:T(8,128)(2,1)}), bf16[8,60,2048]{2,1,0:T(8,128)(2,1)S(1)}, u32[]{:S(2)}, u32[]{:S(2)}) %all-to-all-start) | async-done | bytes 1966112 | tf_op jit(solution)/shard_map/all_to_all | solution.py:189
  733.6 6.3 fusion.28
  744.9 4.7 all-to-all-start.1
  749.9 47.4 %all-to-all-done.1 = bf16[8,60,2048]{2,1,0:T(8,128)(2,1)} async-done(((bf16[8,60,2048]{2,1,0:T(8,128)(2,1)}), bf16[8,60,2048]{2,1,0:T(8,128)(2,1)}, u32[]{:S(2)}, u32[]{:S(2)}) %all-to-all-start.1) | async-done | bytes 1966112 | tf_op jit(solution)/shard_map/all_to_all | solution.py:192
  (203 shorter events, 187.3 us)
Async XLA Ops:
  7.2 316.5 %all-gather.17.cloned.1.call-start = ((), (), s32[]{:S(2)}) async-start(), calls=%async_computation.5 | async-start | bytes 9437184 | tf_op jit(solution)/shard_map/all_gather | solution.py:25
  8.1 8.8 %collective-permute-start = (bf16[3,4096]{1,0:T(4,128)(2,1)S(1)}, bf16[3,4096]{1,0:T(4,128)(2,1)S(1)}, u32[]{:S(2)}, u32[]{:S(2)}) collective-permute-start(bf16[3,4096]{1,0:T(4,128)(2,1)S(1)} %slice.60), channel_id=1, source_target_pairs={{0,1},{1,2},{2,3},{3,4},{4,5},{5,6},{6,7},{7,8},{8,9},{9,10},{10,1... | collective-permute-start | bytes 73736 | tf_op jit(solution)/shard_map/ppermute | solution.py:20
  24.7 3.4 copy-start.11
  24.7 165.3 %slice-start = ((f32[128,4096]{0,1:T(8,128)}), f32[128,2048]{0,1:T(8,128)S(1)}, s32[]{:S(2)}) async-start(f32[128,4096]{0,1:T(8,128)} %copy-done.2), calls=%async_computation.8 | async-start | bytes 2097152 | tf_op jit(solution)/shard_map/slice | solution.py:53
  195.3 3.4 copy-start.13
  198.2 250.7 %all-gather.15.cloned.1.call-start = ((), (), s32[]{:S(2)}) async-start(), calls=%async_computation.4 | async-start | bytes 9437184 | tf_op jit(solution)/shard_map/all_gather | solution.py:25
  203.9 402.5 %all-gather.21.cloned.1.call-start = ((), (), s32[]{:S(2)}) async-start(), calls=%async_computation.7 | async-start | bytes 5242880 | tf_op jit(solution)/shard_map/all_gather | solution.py:25
  528.1 4.9 copy-start.1
  573.6 68.8 %all-gather.19.cloned.1.call-start = ((), (), s32[]{:S(2)}) async-start(), calls=%async_computation.6 | async-start | bytes 5242880 | tf_op jit(solution)/shard_map/all_gather | solution.py:25
  576.9 2.8 copy-start.19
  579.0 5.3 copy-start.16
  579.1 154.6 %all-gather.11.cloned.1.call-start = ((), (), s32[]{:S(2)}) async-start(), calls=%async_computation.2 | async-start | bytes 5242880 | tf_op jit(solution)/shard_map/all_gather | solution.py:186
  580.2 7.4 copy-start.12
  585.3 5.6 copy-start
  663.9 3.5 copy-start.4
  667.4 2.4 copy-start.6
  667.4 2.4 copy-start.8
  669.7 2.3 copy-start.15
  672.1 2.0 copy-start.14
  675.1 132.4 %copy-start.9 = (bf16[128,2048]{1,0:T(8,128)(2,1)}, bf16[128,2048]{1,0:T(8,128)(2,1)S(1)}, u32[]{:S(2)}) copy-start(bf16[128,2048]{1,0:T(8,128)(2,1)S(1)} %copy.117) | copy-start | bytes 1572868
  677.6 54.5 %all-to-all-start = ((bf16[8,60,2048]{2,1,0:T(8,128)(2,1)}), bf16[8,60,2048]{2,1,0:T(8,128)(2,1)S(1)}, u32[]{:S(2)}, u32[]{:S(2)}) async-start(bf16[8,60,2048]{2,1,0:T(8,128)(2,1)} %reshape.207), calls=%async_computation | async-start | bytes 4194304 | tf_op jit(solution)/shard_map/all_to_all | solution.py:189
  683.5 56.5 %all-gather.13.cloned.1.call-start = ((), (), s32[]{:S(2)}) async-start(), calls=%async_computation.3 | async-start | bytes 2621440 | tf_op jit(solution)/shard_map/all_gather | solution.py:187
  744.9 4.9 copy-start.20
  744.9 52.5 %all-to-all-start.1 = ((bf16[8,60,2048]{2,1,0:T(8,128)(2,1)}), bf16[8,60,2048]{2,1,0:T(8,128)(2,1)}, u32[]{:S(2)}, u32[]{:S(2)}) async-start(bf16[8,60,2048]{2,1,0:T(8,128)(2,1)} %reshape.209), calls=%async_computation.1 | async-start | bytes 4194304 | tf_op jit(solution)/shard_map/all_to_all | solution.py:192
  (8 other events, 11.1 us)
Sparse Core Ops, SparseCore 0:
  198.3 125.2 all-gather.16
  325.8 123.1 all-gather.14
  573.7 32.6 all-gather.20
  607.8 34.4 all-gather.18
  643.7 34.4 all-gather.10
  685.5 23.0 all-gather.12
where the time goes:
time: 827 us; the launch traced here: 816 us
  waiting for transfers between devices  384 us (46%)
  other arithmetic  171 us (21%)
  matrix products  154 us (19%)
  local copies, waits for them, and re-layouts  75.2 us (9%)
  starting transfers between devices  15.9 us (2%)
  between operations  14.9 us (2%)
    all_gather x4, waiting for transfers between devices, entering(): pieces = jax.tree.map(lambda part: lax.all_gather(part, axis), value)  287 us
    another operation x1, other arithmetic, local_terms(): lax.linalg.triangular_solve(identity_t[None] + mixing, identity_t[None] *...  159 us
    dot_general x20, matrix products, compose(): jnp.einsum('hvj,hjk->hvk', first_add, second_map, precision=precise)  71.8 us
    all_to_all x1, waiting for transfers between devices, shards(): lax.all_to_all(send_rows, 'ep', split_axis=0, concat_axis=0, tiled=True)  48.1 us
    all_to_all x1, waiting for transfers between devices, shards(): lax.all_to_all(result_rows, 'ep', split_axis=0, concat_axis=0, tiled=True)  47.4 us
    dot_general x16, matrix products, compose(): jnp.einsum('hij,hjk->hik', first_map, second_map, precision=precise)  44.3 us
  transfers between devices with their start and end apart: 9, of which 6 were waited for; matrix products, arithmetic and copies ran while one was open for 9% of the time, Pallas kernels for 0%

commit v1 on v0

--- a/solution.py
+++ b/solution.py
@@ -189,7 +189,15 @@
     slot_rows = lax.all_to_all(send_rows, "ep", split_axis=0, concat_axis=0, tiled=True)
     flat_rows = slot_rows.reshape(-1, width)
     result_rows = expert_mlp(flat_rows, whole_in[0], whole_out[0]).reshape(slot_rows.shape)
-    returned = lax.all_to_all(result_rows, "ep", split_axis=0, concat_axis=0, tiled=True)
+    ways, here = (lax.axis_size("ep"), lax.axis_index("ep"))
+    width_2 = result_rows.shape[0] // ways
+    turned = jnp.roll(result_rows, -here * width_2, axis=0)
+    got = [lax.slice_in_dim(turned, 0, width_2, axis=0)]
+    for far in range(1, ways):
+        sent = lax.slice_in_dim(turned, far * width_2, (far + 1) * width_2, axis=0)
+        got.append(lax.ppermute(sent, "ep", [(d, (d + far) % ways) for d in range(ways)]))
+    line = jnp.concatenate(got[::-1], axis=0)
+    returned = jnp.roll(line, (here + 1) * got[0].shape[0], axis=0)
     returned_flat = returned.reshape(slot_count, width)
     picked_rows = returned_flat[slot_ids].reshape(row_count, TOPK, width)
     combined = jnp.einsum("tk,tkd->td", route_gates, picked_rows.astype(jnp.float32))

time: 827 us -> 826 us (level)
  waiting for transfers between devices: 384 us -> 372 us
    all_to_all x1 -> x0, waiting for transfers between devices: 47.4 us -> none  [shards(): lax.all_to_all(result_rows, 'ep', split_axis=0, concat_axis=0, tiled=True)]
    ppermute x0 -> x7, waiting for transfers between devices: none -> 38 us  [shards(): lax.ppermute(sent, 'ep', [(d, (d + far) % ways) for d in range(ways)])]
  transfers between devices with their start and end apart: 9 -> 15, of which waited for: 6 -> 10; matrix products, arithmetic and copies ran while one was open for 9% -> 10% of each run, Pallas kernels for 0% -> 0%
where the time goes in v1:
time: 826 us; the launch traced here: 817 us
  waiting for transfers between devices  372 us (45%)
  other arithmetic  175 us (21%)
  matrix products  153 us (19%)
  local copies, waits for them, and re-layouts  81.6 us (10%)
  starting transfers between devices  19 us (2%)
  between operations  15.1 us (2%)
    all_gather x4, waiting for transfers between devices, entering(): pieces = jax.tree.map(lambda part: lax.all_gather(part, axis), value)  285 us
    another operation x1, other arithmetic, local_terms(): lax.linalg.triangular_solve(identity_t[None] + mixing, identity_t[None] *...  158 us
    dot_general x20, matrix products, compose(): jnp.einsum('hvj,hjk->hvk', first_add, second_map, precision=precise)  71.8 us
    all_to_all x1, waiting for transfers between devices, shards(): lax.all_to_all(send_rows, 'ep', split_axis=0, concat_axis=0, tiled=True)  48.1 us
    dot_general x16, matrix products, compose(): jnp.einsum('hij,hjk->hik', first_map, second_map, precision=precise)  44.3 us
    ppermute x7, waiting for transfers between devices, shards(): lax.ppermute(sent, 'ep', [(d, (d + far) % ways) for d in range(ways)])  38 us
  transfers between devices with their start and end apart: 15, of which 10 were waited for; matrix products, arithmetic and copies ran while one was open for 10% of the time, Pallas kernels for 0%

profile of v1, /device:TPU:0, one launch (start us, length us, event | category | flops | bytes accessed | tf_op | source)
XLA Modules:
  0.0 817.0 jit_solution(7295103470918051376)
XLA Ops:
  8.1 4.8 collective-permute-start
  18.4 4.6 divide_multiply_fusion
  29.7 158.0 %custom-call.3 = f32[16,1,128,128]{2,3,1,0:T(8,128)} custom-call(f32[16,1,128,128]{3,2,1,0:T(8,128)S(1)} %fusion.41), custom_call_target="InvertDiagBlocksLowerTriangular" | custom-call | tf_op jit(solution)/shard_map/triangular_solve | solution.py:72
  205.4 117.6 %all-gather.15.cloned.1.call-done = f32[128,128,128]{2,1,0:T(8,128)} async-done(((f32[16,128,128]{2,1,0:T(8,128)}), f32[128,128,128]{2,1,0:T(8,128)}) %all-gather.15.cloned.1.call-update) | async-done | bytes 8388624 | tf_op jit(solution)/shard_map/all_gather | solution.py:25
  323.0 7.7 rev.6
  330.7 117.5 %all-gather.17.cloned.1.call-done = f32[128,128,128]{2,1,0:T(8,128)} async-done(((f32[16,128,128]{2,1,0:T(8,128)}), f32[128,128,128]{2,1,0:T(8,128)}) %all-gather.17.cloned.1.call-update) | async-done | bytes 8388624 | tf_op jit(solution)/shard_map/all_gather | solution.py:25
  448.3 7.7 rev.7
  456.1 71.6 %while.46 = (s32[]{:T(128)}, f32[16,128,128]{1,2,0:T(8,128)S(1)}, f32[16,128,128]{1,2,0:T(8,128)}, s32[]{:T(128)}, f32[8,16,128,128]{3,2,1,0:T(8,128)}, /*index=5*/f32[8,16,128,128]{3,2,1,0:T(8,128)}, s32[]{:T(128)}, s32[]{:T(128)}) while((s32[]{:T(128)}, f32[16,128,128]{1,2,0:T(8,128)S(1)}, f32[16,128,128]{1,2,0:T(8,128)}, ...), condition=%wide.region_4.5_spmd.clone, body=%wide.region_3.4_spmd.clone.sunk | while | flops 806617088 | bytes 17828460 | solution.py:37
  469.4 4.1 fusion.121
  479.6 4.1 fusion.121
  527.6 4.8 convolution_add_fusion.2
  532.5 37.2 %while.47 = (s32[]{:T(128)}, f32[16,128,128]{2,1,0:T(8,128)S(1)}, f32[16,128,128]{2,1,0:T(8,128)S(1)}, s32[]{:T(128)}, f32[8,16,128,128]{3,2,1,0:T(8,128)}, /*in...) while((s32[]{:T(128)}, f32[16,128,128]{2,1,0:T(8,128)S(1)}, f32[16,128,128]{2,1,0:T(8,128)S(1)}, ...), condition=%wide.region_6.7_spmd.clone, body=%wide.region_5.6_spmd.clone.sunk | while | flops 806354944 | bytes 10486890 | solution.py:37
  591.9 14.0 %all-gather.21.cloned.1.call-done = f32[64,128,128]{2,1,0:T(8,128)} async-done(((f32[16,128,128]{2,1,0:T(8,128)}), f32[64,128,128]{2,1,0:T(8,128)}) %all-gather.21.cloned.1.call-update) | async-done | bytes 4194320 | tf_op jit(solution)/shard_map/all_gather | solution.py:25
  605.9 36.0 %all-gather.19.cloned.1.call-done = f32[64,128,128]{2,1,0:T(8,128)} async-done(((f32[16,128,128]{2,1,0:T(8,128)}), f32[64,128,128]{2,1,0:T(8,128)}) %all-gather.19.cloned.1.call-update) | async-done | bytes 4194320 | tf_op jit(solution)/shard_map/all_gather | solution.py:25
  641.9 21.3 %while.48 = (s32[]{:T(128)}, f32[16,128,128]{1,2,0:T(8,128)}, s32[]{:T(128)}, f32[4,16,128,128]{3,2,1,0:T(8,128)}, f32[4,16,128,128]{3,2,1,0:T(8,128)}, /*index=5*/s32[]{:T(128)}, s32[]{:T(128)}) while((s32[]{:T(128)}, f32[16,128,128]{1,2,0:T(8,128)}, s32[]{:T(128)}, f32[4,16,128,128]{3,2,1,0:T(8,128)}, ...), condition=%wide.region_8.9_spmd.clone, body=%wide.region_7.8_spmd.clone.sunk | while | flops 403701760 | bytes 11536483 | solution.py:37
  644.8 4.1 fusion.128
  651.9 4.2 fusion.128
  659.0 4.1 fusion.128
  677.1 5.8 all-to-all-start
  683.5 48.1 %all-to-all-done = bf16[8,60,2048]{2,1,0:T(8,128)(2,1)S(1)} async-done(((bf16[8,60,2048]{2,1,0:T(8,128)(2,1)}), bf16[8,60,2048]{2,1,0:T(8,128)(2,1)S(1)}, u32[]{:S(2)}, u32[]{:S(2)}) %all-to-all-start) | async-done | bytes 1966112 | tf_op jit(solution)/shard_map/all_to_all | solution.py:189
  733.3 6.3 fusion.28
  751.1 4.2 collective-permute-start.4
  759.0 4.9 collective-permute-done.2
  768.9 26.0 %collective-permute-done.4 = bf16[1,60,2048]{2,1,0:T(8,128)(2,1)S(1)} collective-permute-done((bf16[1,60,2048]{2,1,0:T(8,128)(2,1)}, bf16[1,60,2048]{2,1,0:T(8,128)(2,1)S(1)}, u32[]{:S(2)}, u32[]{:S(2)}) %collective-permute-start.4) | collective-permute-done | bytes 245792 | tf_op jit(solution)/shard_map/ppermute | solution.py:198
  (225 shorter events, 212.1 us)
Async XLA Ops:
  7.2 315.8 %all-gather.15.cloned.1.call-start = ((), (), s32[]{:S(2)}) async-start(), calls=%async_computation.3 | async-start | bytes 9437184 | tf_op jit(solution)/shard_map/all_gather | solution.py:25
  8.1 9.0 %collective-permute-start = (bf16[3,4096]{1,0:T(4,128)(2,1)S(1)}, bf16[3,4096]{1,0:T(4,128)(2,1)S(1)}, u32[]{:S(2)}, u32[]{:S(2)}) collective-permute-start(bf16[3,4096]{1,0:T(4,128)(2,1)S(1)} %slice.84), channel_id=1, source_target_pairs={{0,1},{1,2},{2,3},{3,4},{4,5},{5,6},{6,7},{7,8},{8,9},{9,10},{10,1... | collective-permute-start | bytes 73736 | tf_op jit(solution)/shard_map/ppermute | solution.py:20
  24.2 3.1 copy-start.17
  191.1 3.5 copy-start.6
  197.6 250.7 %all-gather.17.cloned.1.call-start = ((), (), s32[]{:S(2)}) async-start(), calls=%async_computation.4 | async-start | bytes 9437184 | tf_op jit(solution)/shard_map/all_gather | solution.py:25
  205.3 400.7 %all-gather.21.cloned.1.call-start = ((), (), s32[]{:S(2)}) async-start(), calls=%async_computation.6 | async-start | bytes 5242880 | tf_op jit(solution)/shard_map/all_gather | solution.py:25
  527.6 4.9 copy-start.1
  573.1 68.8 %all-gather.19.cloned.1.call-start = ((), (), s32[]{:S(2)}) async-start(), calls=%async_computation.5 | async-start | bytes 5242880 | tf_op jit(solution)/shard_map/all_gather | solution.py:25
  578.8 5.3 copy-start.16
  578.8 154.5 %all-gather.11.cloned.1.call-start = ((), (), s32[]{:S(2)}) async-start(), calls=%async_computation.1 | async-start | bytes 5242880 | tf_op jit(solution)/shard_map/all_gather | solution.py:186
  579.9 7.3 copy-start.13
  585.0 5.5 copy-start
  663.3 3.5 copy-start.3
  674.5 134.2 %copy-start.10 = (bf16[128,2048]{1,0:T(8,128)(2,1)}, bf16[128,2048]{1,0:T(8,128)(2,1)S(1)}, u32[]{:S(2)}) copy-start(bf16[128,2048]{1,0:T(8,128)(2,1)S(1)} %copy.117) | copy-start | bytes 1572868
  677.1 54.5 %all-to-all-start = ((bf16[8,60,2048]{2,1,0:T(8,128)(2,1)}), bf16[8,60,2048]{2,1,0:T(8,128)(2,1)S(1)}, u32[]{:S(2)}, u32[]{:S(2)}) async-start(bf16[8,60,2048]{2,1,0:T(8,128)(2,1)} %reshape.207), calls=%async_computation | async-start | bytes 4194304 | tf_op jit(solution)/shard_map/all_to_all | solution.py:189
  682.9 56.8 %all-gather.13.cloned.1.call-start = ((), (), s32[]{:S(2)}) async-start(), calls=%async_computation.2 | async-start | bytes 2621440 | tf_op jit(solution)/shard_map/all_gather | solution.py:187
  746.9 3.9 copy-start.20
  748.1 9.5 %collective-permute-start.1 = (bf16[1,60,2048]{2,1,0:T(8,128)(2,1)}, bf16[1,60,2048]{2,1,0:T(8,128)(2,1)}, u32[]{:S(2)}, u32[]{:S(2)}) collective-permute-start(bf16[1,60,2048]{2,1,0:T(8,128)(2,1)} %get-tuple-element.476), channel_id=1, source_target_pairs={{0,7},{1,0},{2,1},{3,2},{4,3},{5,4},{6,5},{7,6},{8,15},{9,8},{10,9... | collective-permute-start | bytes 737288 | tf_op jit(solution)/shard_map/ppermute | solution.py:198
  750.7 13.2 %collective-permute-start.2 = (bf16[1,60,2048]{2,1,0:T(8,128)(2,1)}, bf16[1,60,2048]{2,1,0:T(8,128)(2,1)}, u32[]{:S(2)}, u32[]{:S(2)}) collective-permute-start(bf16[1,60,2048]{2,1,0:T(8,128)(2,1)} %get-tuple-element.475), channel_id=1, source_target_pairs={{0,6},{1,7},{2,0},{3,1},{4,2},{5,3},{6,4},{7,5},{8,14},{9,15},{10,... | collective-permute-start | bytes 737288 | tf_op jit(solution)/shard_map/ppermute | solution.py:198
  751.0 17.9 %collective-permute-start.3 = (bf16[1,60,2048]{2,1,0:T(8,128)(2,1)}, bf16[1,60,2048]{2,1,0:T(8,128)(2,1)S(1)}, u32[]{:S(2)}, u32[]{:S(2)}) collective-permute-start(bf16[1,60,2048]{2,1,0:T(8,128)(2,1)} %get-tuple-element.474), channel_id=1, source_target_pairs={{0,5},{1,6},{2,7},{3,0},{4,1},{5,2},{6,3},{7,4},{8,13},{9,14},{10,... | collective-permute-start | bytes 737288 | tf_op jit(solution)/shard_map/ppermute | solution.py:198
  751.1 43.8 %collective-permute-start.4 = (bf16[1,60,2048]{2,1,0:T(8,128)(2,1)}, bf16[1,60,2048]{2,1,0:T(8,128)(2,1)S(1)}, u32[]{:S(2)}, u32[]{:S(2)}) collective-permute-start(bf16[1,60,2048]{2,1,0:T(8,128)(2,1)} %get-tuple-element.473), channel_id=1, source_target_pairs={{0,4},{1,5},{2,6},{3,7},{4,0},{5,1},{6,2},{7,3},{8,12},{9,13},{10,... | collective-permute-start | bytes 737288 | tf_op jit(solution)/shard_map/ppermute | solution.py:198
  755.3 41.0 %collective-permute-start.5 = (bf16[1,60,2048]{2,1,0:T(8,128)(2,1)}, bf16[1,60,2048]{2,1,0:T(8,128)(2,1)S(1)}, u32[]{:S(2)}, u32[]{:S(2)}) collective-permute-start(bf16[1,60,2048]{2,1,0:T(8,128)(2,1)} %get-tuple-element.472), channel_id=1, source_target_pairs={{0,3},{1,4},{2,5},{3,6},{4,7},{5,0},{6,1},{7,2},{8,11},{9,12},{10,... | collective-permute-start | bytes 737288 | tf_op jit(solution)/shard_map/ppermute | solution.py:198
  757.6 38.7 %collective-permute-start.6 = (bf16[1,60,2048]{2,1,0:T(8,128)(2,1)}, bf16[1,60,2048]{2,1,0:T(8,128)(2,1)S(1)}, u32[]{:S(2)}, u32[]{:S(2)}) collective-permute-start(bf16[1,60,2048]{2,1,0:T(8,128)(2,1)} %get-tuple-element.471), channel_id=1, source_target_pairs={{0,2},{1,3},{2,4},{3,5},{4,6},{5,7},{6,0},{7,1},{8,10},{9,11},{10,... | collective-permute-start | bytes 737288 | tf_op jit(solution)/shard_map/ppermute | solution.py:198
  763.9 32.5 %collective-permute-start.7 = (bf16[1,60,2048]{2,1,0:T(8,128)(2,1)S(1)}, bf16[1,60,2048]{2,1,0:T(8,128)(2,1)S(1)}, u32[]{:S(2)}, u32[]{:S(2)}) collective-permute-start(bf16[1,60,2048]{2,1,0:T(8,128)(2,1)S(1)} %get-tuple-element.470), channel_id=1, source_target_pairs={{0,1},{1,2},{2,3},{3,4},{4,5},{5,6},{6,7},{7,0},{8,9},{9,10},{10,1... | collective-permute-start | bytes 737288 | tf_op jit(solution)/shard_map/ppermute | solution.py:198
  (13 other events, 22.2 us)
Sparse Core Ops, SparseCore 0:
  197.7 125.2 all-gather.14
  325.1 123.1 all-gather.16
  573.2 32.6 all-gather.20
  607.4 34.5 all-gather.18
  643.3 34.4 all-gather.10
  684.9 23.0 all-gather.12
